TPU v7x, 32 devices: a whole 2x2x4 slice. The times are simulated.
32 devices in a mesh: row: 4 (over x, core), col: 8 (over z, y).
Axes of the slice: x: 2, y: 2, z: 4, core: 2. Of those that a mesh axis runs over, the one named last changes fastest.
Arguments:
- masters: float32 [128, 4096], P('col'), may hold values from -6 to 6
- inst_master: int32 [64, 128], P('row', 'col'), may hold values from 0 to 127
- inst_orient: int32 [64, 128], P('row', 'col'), may hold values from 0 to 3
- owner_map: int32 [128], replicated, may hold values from 0 to 127, each once
- tile_free: float32 [4096, 8192], P('row', 'col'), may hold values from -3 to 3
- target: float32 [4096, 8192], P('row', 'col'), may hold values from 0 to 1
- kernel_spectra: float32 [2, 128, 8, 128], replicated, may hold values from -6 to 6
- socs_weights: float32 [8], replicated, may hold values from 0.05 to 1
Outputs:
- resist: float32 [4096, 8192], P('row', 'col')
- new_mask: float32 [4096, 8192], P('row', 'col')
- masters_out: float32 [128, 4096], P('col')
Inputs may be any that keep to these rules, and one draw needn't show every extreme that they name: `inst_orient`: bit 0 reverses a cell's rows, bit 1 its columns. `owner_map`: each storage row is used by exactly one master; storage row r lies on index r // 16 of col.
All inputs are finite; a program needn't handle non-finite values.
Results may differ from a plain program's by a relative error of at most 0.0092.
Values may be sent and summed in bfloat16 or wider, within the bound.
A program may use at most 128 MiB of HBM per device.

v0:
```python
import math
import jax
import jax.numpy as jnp
from jax import lax
from jax.sharding import PartitionSpec as P

TILE = 512
TPD = 2
HALO = 64
CELL = 64
step_free = 1.0
step_master = 0.05
resist_gain = 2.0
resist_level = 1.8


def padded_2(value, sides, width):
    for axis, dim in sides:
        peers, length = (lax.axis_size(axis), value.shape[dim])
        up = [(i, (i + 1) % peers) for i in range(peers - 1)]
        down = [(j, i) for i, j in up]
        last = lax.slice_in_dim(value, length - width, length, axis=dim)
        initial = lax.slice_in_dim(value, 0, width, axis=dim)
        before = lax.ppermute(last, axis, up)
        after = lax.ppermute(initial, axis, down)
        value = jnp.concatenate([before, value, after], axis=dim)
    return value


def dot_plain(left, right):
    return jnp.dot(left, right, preferred_element_type=jnp.float32)


def dot_right_t(left, right):
    return lax.dot_general(
        left, right, (((1,), (1,)), ((), ())), preferred_element_type=jnp.float32
    )


def dot_left_t(left, right):
    return lax.dot_general(
        left, right, (((0,), (0,)), ((), ())), preferred_element_type=jnp.float32
    )


def tables(pad_side, band_side):
    freqs = jnp.arange(band_side, dtype=jnp.int32) - band_side // 2
    pixels = jnp.arange(pad_side, dtype=jnp.int32)
    phases = freqs[:, None] * pixels[None, :] % pad_side
    angles = phases.astype(jnp.float32) * (2.0 * math.pi / pad_side)
    return (jnp.cos(angles).astype(jnp.bfloat16), jnp.sin(angles).astype(jnp.bfloat16))


def tile_step(padded, target, spectra, weights, halo_side):
    pad_side = padded.shape[0]
    band_side = spectra.shape[1]
    kernels = spectra.shape[2]
    tile_side = pad_side - 2 * halo_side
    cos_full, sin_full = tables(pad_side, band_side)
    cos_in = cos_full[:, halo_side : halo_side + tile_side]
    sin_in = sin_full[:, halo_side : halo_side + tile_side]
    forw_re = dot_plain(cos_full, padded).astype(jnp.bfloat16)
    forw_im = (-dot_plain(sin_full, padded)).astype(jnp.bfloat16)
    spec_re = (dot_right_t(forw_re, cos_full) - dot_right_t(forw_im, sin_full)) / pad_side
    spec_im = (-dot_right_t(forw_re, sin_full) - dot_right_t(forw_im, cos_full)) / pad_side
    kern_re = spectra[0]
    kern_im = spectra[1]
    amp_re = (kern_re * spec_re[:, None, :] - kern_im * spec_im[:, None, :]).astype(jnp.bfloat16)
    amp_im = (kern_re * spec_im[:, None, :] + kern_im * spec_re[:, None, :]).astype(jnp.bfloat16)
    amp_re = amp_re.reshape(band_side, kernels * band_side)
    amp_im = amp_im.reshape(band_side, kernels * band_side)
    half_re = (dot_left_t(cos_in, amp_re) - dot_left_t(sin_in, amp_im)).astype(jnp.bfloat16)
    half_im = (dot_left_t(cos_in, amp_im) + dot_left_t(sin_in, amp_re)).astype(jnp.bfloat16)
    half_re = half_re.reshape(tile_side * kernels, band_side)
    half_im = half_im.reshape(tile_side * kernels, band_side)
    field_re = (dot_plain(half_re, cos_in) - dot_plain(half_im, sin_in)) / band_side
    field_im = (dot_plain(half_re, sin_in) + dot_plain(half_im, cos_in)) / band_side
    field_re = field_re.reshape(tile_side, kernels, tile_side)
    field_im = field_im.reshape(tile_side, kernels, tile_side)
    scaled = weights[None, :, None]
    intensity = jnp.sum(scaled * (field_re * field_re + field_im * field_im), axis=1)
    resist = jax.nn.sigmoid(resist_gain * (intensity - resist_level))
    slopes = 2.0 * (resist - target) * resist_gain * resist * (1.0 - resist)
    back_re = (2.0 / band_side * scaled * slopes[:, None, :] * field_re).astype(jnp.bfloat16)
    back_im = (2.0 / band_side * scaled * slopes[:, None, :] * field_im).astype(jnp.bfloat16)
    back_re = back_re.reshape(tile_side * kernels, tile_side)
    back_im = back_im.reshape(tile_side * kernels, tile_side)
    bhalf_re = (dot_right_t(back_re, cos_in) + dot_right_t(back_im, sin_in)).astype(jnp.bfloat16)
    bhalf_im = (dot_right_t(back_im, cos_in) - dot_right_t(back_re, sin_in)).astype(jnp.bfloat16)
    bhalf_re = bhalf_re.reshape(tile_side, kernels * band_side)
    bhalf_im = bhalf_im.reshape(tile_side, kernels * band_side)
    bamp_re = (dot_plain(cos_in, bhalf_re) + dot_plain(sin_in, bhalf_im)).reshape(
        band_side, kernels, band_side
    )
    bamp_im = (dot_plain(cos_in, bhalf_im) - dot_plain(sin_in, bhalf_re)).reshape(
        band_side, kernels, band_side
    )
    bspec_re = (jnp.sum(kern_re * bamp_re + kern_im * bamp_im, axis=1) / pad_side).astype(
        jnp.bfloat16
    )
    bspec_im = (jnp.sum(kern_re * bamp_im - kern_im * bamp_re, axis=1) / pad_side).astype(
        jnp.bfloat16
    )
    bforw_re = (dot_plain(bspec_re, cos_in) - dot_plain(bspec_im, sin_in)).astype(jnp.bfloat16)
    bforw_im = (-dot_plain(bspec_re, sin_in) - dot_plain(bspec_im, cos_in)).astype(jnp.bfloat16)
    gradient = dot_left_t(cos_in, bforw_re) - dot_left_t(sin_in, bforw_im)
    return (resist, gradient)


def orient_cells(cells, orient):
    flip_first = orient % 2 == 1
    flip_second = orient // 2 == 1
    cells = jnp.where(flip_first[..., None, None], cells[..., ::-1, :], cells)
    cells = jnp.where(flip_second[..., None, None], cells[..., :, ::-1], cells)
    return cells


def assemble(master_rows, slots, orient, cell_side):
    grid_rows, grid_cols = slots.shape
    cells = jnp.take(master_rows, slots.reshape(-1), axis=0)
    cells = cells.reshape(grid_rows, grid_cols, cell_side, cell_side)
    cells = orient_cells(cells, orient)
    return cells.transpose(0, 2, 1, 3).reshape(grid_rows * cell_side, grid_cols * cell_side)


def cells_of(image, orient, cell_side):
    grid_rows, grid_cols = orient.shape
    cells = image.reshape(grid_rows, cell_side, grid_cols, cell_side).transpose(0, 2, 1, 3)
    cells = orient_cells(cells, orient)
    return cells.reshape(grid_rows * grid_cols, cell_side * cell_side)


def smooth(master_rows, cell_side):
    grids = master_rows.reshape(-1, cell_side, cell_side)
    framed = jnp.pad(grids, ((0, 0), (1, 1), (1, 1)))
    beside_all = (
        framed[:, 2:, 1:-1] + framed[:, :-2, 1:-1] + framed[:, 1:-1, 2:] + framed[:, 1:-1, :-2]
    )
    return (0.5 * grids + 0.125 * beside_all).reshape(master_rows.shape)


def stitch_local(tiles):
    return tiles.reshape(TPD, TPD, TILE, TILE).transpose(0, 2, 1, 3).reshape(TPD * TILE, TPD * TILE)


def per_device(
    masters, inst_master, inst_orient, owner_map, tile_free, target, kernel_spectra, socs_weights
):
    stored = masters.shape[0]
    everything = lax.all_gather(masters, "col", axis=0, tiled=True)
    total_masters = everything.shape[0]
    matches = inst_master[..., None] == jnp.arange(total_masters, dtype=jnp.int32)
    slots = jnp.sum(jnp.where(matches, owner_map, 0), axis=-1)
    flat_slots = slots.reshape(-1)
    col_index = lax.axis_index("col")
    free_field = tile_free
    pad_side = TILE + 2 * HALO
    shading = jnp.tanh(assemble(everything, slots, inst_orient, CELL) + free_field)
    mask_block = shading.astype(jnp.bfloat16)
    padded = padded_2(mask_block, (("row", 0), ("col", 1)), HALO)

    def one_tile(tile_index):
        row_at = tile_index // TPD
        col_at = tile_index % TPD
        window = lax.dynamic_slice(padded, (row_at * TILE, col_at * TILE), (pad_side, pad_side))
        goal_tile = lax.dynamic_slice(target, (row_at * TILE, col_at * TILE), (TILE, TILE))
        return tile_step(window, goal_tile, kernel_spectra, socs_weights, HALO)

    resist_tiles, grad_tiles = lax.map(one_tile, jnp.arange(TPD * TPD, dtype=jnp.int32))
    resist = stitch_local(resist_tiles)
    grad_param = stitch_local(grad_tiles) * (1.0 - shading * shading)
    free_field = free_field - step_free * grad_param
    cell_grads = cells_of(grad_param, inst_orient, CELL)
    wanted = jnp.arange(total_masters, dtype=jnp.int32)
    selector = (flat_slots[None, :] == wanted[:, None]).astype(jnp.float32)
    whole_sum = lax.psum(
        jnp.dot(
            selector,
            cell_grads,
            precision=lax.Precision.HIGHEST,
            preferred_element_type=jnp.float32,
        ).astype(jnp.bfloat16),
        "row",
    )
    summed = lax.psum_scatter(whole_sum, "col", scatter_dimension=0, tiled=True).astype(jnp.float32)
    own_rows = lax.dynamic_slice_in_dim(everything, col_index * stored, stored, 0)
    fresh = smooth(own_rows - step_master * summed, CELL)
    everything = lax.all_gather(fresh.astype(jnp.bfloat16), "col", axis=0, tiled=True).astype(
        fresh.dtype
    )
    new_mask = jnp.tanh(assemble(everything, slots, inst_orient, CELL) + free_field)
    masters_out = lax.dynamic_slice_in_dim(everything, col_index * stored, stored, 0)
    return (resist, new_mask, masters_out)


def solution(mesh):
    in_specs = (
        P("col", None),
        P("row", "col"),
        P("row", "col"),
        P(),
        P("row", "col"),
        P("row", "col"),
        P(),
        P(),
    )
    out_specs = (P("row", "col"), P("row", "col"), P("col", None))
    return jax.shard_map(
        per_device, mesh=mesh, in_specs=in_specs, out_specs=out_specs, check_vma=False
    )
```

profile of v0, /device:TPU:0, one launch (start us, length us, event | category | flops | bytes accessed | tf_op | source)
XLA Modules:
  0.0 786.2 jit_solution(12624637121962711433)
XLA Ops:
  10.0 52.0 %all-gather.3.cloned.1.call-done = f32[128,4096]{1,0:T(8,128)} async-done(((f32[16,4096]{1,0:T(8,128)}), f32[128,4096]{1,0:T(8,128)}) %all-gather.3.cloned.1.call-update) | async-done | bytes 2097168 | tf_op jit(solution)/shard_map/all_gather | solution.py:150
  74.0 8.1 %reshape.201 = f32[16,16,64,64]{3,2,1,0:T(8,128)} reshape(f32[256,4096]{1,0:T(8,128)} %broadcast_select_fusion.5) | data formatting | bytes 8388608 | tf_op jit(solution)/shard_map/reshape | solution.py:121
  82.1 12.0 %rev.18 = f32[16,16,64,64]{3,2,1,0:T(8,128)} reverse(f32[16,16,64,64]{3,2,1,0:T(8,128)} %reshape.201), dimensions={2} | reverse | bytes 8388608 | tf_op jit(solution)/shard_map/rev | solution.py:113
  94.1 9.8 %broadcast_select_fusion.2 = f32[16,16,64,64]{3,2,1,0:T(8,128)} fusion(f32[16,16,64,64]{3,2,1,0:T(8,128)} %rev.18, f32[16,16,64,64]{3,2,1,0:T(8,128)} %reshape.201, pred[16,16]{1,0:T(8,128)(4,1)S(1)} %get-tuple-element.182), kind=kLoop, calls=%fused_computation.136 | loop fusion | flops 1048576 | bytes 12583168 | tf_op jit(solution)/shard_map/jit(_where)/select_n | solution.py:113
  103.9 13.2 %rev.19 = f32[16,16,64,64]{3,2,1,0:T(8,128)} reverse(f32[16,16,64,64]{3,2,1,0:T(8,128)} %broadcast_select_fusion.2), dimensions={3} | reverse | bytes 8388608 | tf_op jit(solution)/shard_map/rev | solution.py:114
  123.4 9.8 %copy.21 = f32[16,64,16,64]{3,2,1,0:T(8,128)} copy(f32[16,64,16,64]{3,1,2,0:T(8,128)S(1)} %select_bitcast_fusion.1) | data formatting | bytes 8388608 | tf_op jit(solution)/shard_map/transpose | solution.py:123
  133.2 7.6 reshape.202
  171.8 290.4 %while.15 = (s32[]{:T(128)}, f32[4,512,512]{2,1,0:T(8,128)}, f32[4,512,512]{2,1,0:T(8,128)}, f32[8]{0:T(128)S(1)}, f32[2,128,8,128]{3,2,1,0:T(8,128)S(1)}, /*ind...) while((s32[]{:T(128)}, f32[4,512,512]{2,1,0:T(8,128)}, ...), condition=%wide.region_5.7_spmd, body=%wide.region_1.6_spmd.sunk | while | flops 5924732928 | bytes 203478224 | solution.py:169
  481.9 9.2 %copy.45 = f32[16,64,16,64]{3,1,2,0:T(8,128)} copy(f32[16,64,16,64]{3,2,1,0:T(8,128)} %reshape.207) | data formatting | bytes 8388608 | tf_op jit(solution)/shard_map/reshape | solution.py:128
  491.1 11.9 %rev.20 = f32[16,16,64,64]{3,2,1,0:T(8,128)} reverse(f32[16,16,64,64]{3,2,1,0:T(8,128)} %bitcast.205), dimensions={2} | reverse | bytes 8388608 | tf_op jit(solution)/shard_map/rev | solution.py:113
  503.1 11.0 %broadcast_select_fusion.1 = f32[16,16,64,64]{3,2,1,0:T(8,128)} fusion(f32[16,16,64,64]{3,2,1,0:T(8,128)} %rev.20, pred[16,16]{1,0:T(8,128)(4,1)S(1)} %copy-done.8, f32[16,64,16,64]{3,2,1,0:T(8,128)} %reshape.207), kind=kLoop, calls=%fused_computation.135 | loop fusion | flops 1048576 | bytes 12583168 | tf_op jit(solution)/shard_map/jit(_where)/select_n | solution.py:113
  514.0 13.2 %rev.21 = f32[16,16,64,64]{3,2,1,0:T(8,128)} reverse(f32[16,16,64,64]{3,2,1,0:T(8,128)} %broadcast_select_fusion.1), dimensions={3} | reverse | bytes 8388608 | tf_op jit(solution)/shard_map/rev | solution.py:114
  527.2 9.8 %broadcast_select_fusion.3 = f32[16,16,64,64]{3,2,1,0:T(8,128)} fusion(f32[16,16,64,64]{3,2,1,0:T(8,128)} %rev.21, f32[16,16,64,64]{3,2,1,0:T(8,128)} %broadcast_select_fusion.1, pred[16,16]{1,0:T(8,128)(4,1)S(1)} %copy-done.6), kind=kLoop, calls=%fused_computation.137 | loop fusion | flops 1048576 | bytes 12583168 | tf_op jit(solution)/shard_map/jit(_where)/select_n | solution.py:114
  537.1 7.9 %reshape.208 = f32[256,4096]{1,0:T(8,128)} reshape(f32[16,16,64,64]{3,2,1,0:T(8,128)} %broadcast_select_fusion.3) | data formatting | bytes 8388608 | tf_op jit(solution)/shard_map/reshape | solution.py:130
  549.9 67.1 %reduce-scatter.2.cloned.1.call-done = bf16[16,4096]{1,0:T(8,128)(2,1)} async-done(((bf16[128,4096]{1,0:T(8,128)(2,1)}), bf16[16,4096]{1,0:T(8,128)(2,1)}) %reduce-scatter.2.cloned.1.call-update) | async-done | bytes 131088 | tf_op jit(solution)/shard_map/reduce_scatter | solution.py:185
  617.1 33.0 %all-reduce.3.cloned.1.call-done = bf16[16,4096]{1,0:T(8,128)(2,1)} async-done(((bf16[16,4096]{1,0:T(8,128)(2,1)}), bf16[16,4096]{1,0:T(8,128)(2,1)}) %all-reduce.3.cloned.1.call-update) | async-done | bytes 131088 | tf_op jit(solution)/shard_map/psum | solution.py:176
  661.1 32.0 %all-gather.5.cloned.1.call-done = bf16[128,4096]{1,0:T(8,128)(2,1)} async-done(((bf16[16,4096]{1,0:T(8,128)(2,1)}), bf16[128,4096]{1,0:T(8,128)(2,1)}) %all-gather.5.cloned.1.call-update) | async-done | bytes 1048592 | tf_op jit(solution)/shard_map/all_gather | solution.py:188
  704.1 8.1 %reshape.210 = f32[16,16,64,64]{3,2,1,0:T(8,128)} reshape(f32[256,4096]{1,0:T(8,128)} %broadcast_select_fusion.4) | data formatting | bytes 8388608 | tf_op jit(solution)/shard_map/reshape | solution.py:121
  712.2 12.0 %rev.22 = f32[16,16,64,64]{3,2,1,0:T(8,128)} reverse(f32[16,16,64,64]{3,2,1,0:T(8,128)} %reshape.210), dimensions={2} | reverse | bytes 8388608 | tf_op jit(solution)/shard_map/rev | solution.py:113
  724.1 9.8 %broadcast_select_fusion = f32[16,16,64,64]{3,2,1,0:T(8,128)} fusion(f32[16,16,64,64]{3,2,1,0:T(8,128)} %rev.22, f32[16,16,64,64]{3,2,1,0:T(8,128)} %reshape.210, pred[16,16]{1,0:T(8,128)(4,1)S(1)} %copy-done.8), kind=kLoop, calls=%fused_computation.134 | loop fusion | flops 1048576 | bytes 12583168 | tf_op jit(solution)/shard_map/jit(_where)/select_n | solution.py:113
  733.9 13.2 %rev.23 = f32[16,16,64,64]{3,2,1,0:T(8,128)} reverse(f32[16,16,64,64]{3,2,1,0:T(8,128)} %broadcast_select_fusion), dimensions={3} | reverse | bytes 8388608 | tf_op jit(solution)/shard_map/rev | solution.py:114
  753.5 9.8 %copy.25 = f32[16,64,16,64]{3,2,1,0:T(8,128)} copy(f32[16,64,16,64]{3,1,2,0:T(8,128)S(1)} %select_bitcast_fusion) | data formatting | bytes 8388608 | tf_op jit(solution)/shard_map/transpose | solution.py:123
  763.3 7.6 reshape.211
  770.9 8.6 %add_tanh_fusion = f32[1024,1024]{1,0:T(8,128)} fusion(f32[1024,1024]{1,0:T(8,128)} %reshape.211, f32[1024,1024]{1,0:T(8,128)} %param.16, f32[1024,1024]{1,0:T(8,128)} %subtract_multiply_fusion.2), kind=kLoop, calls=%fused_computation.131 | loop fusion | flops 2097152 | bytes 16777216 | tf_op jit(solution)/shard_map/tanh | solution.py:191
  (271 shorter events, 368.1 us)
Async XLA Ops:
  7.2 54.8 %all-gather.3.cloned.1.call-start = ((), (), s32[]{:S(2)}) async-start(), calls=%async_computation.1 | async-start | bytes 2359296 | tf_op jit(solution)/shard_map/all_gather | solution.py:150
  7.9 609.1 %reduce-scatter.2.cloned.1.call-start = ((), (), s32[]{:S(2)}) async-start(), calls=%async_computation.3 | async-start | bytes 1179648 | tf_op jit(solution)/shard_map/reduce_scatter | solution.py:185
  9.2 60.1 %copy-start.11 = (s32[256]{0:T(256)}, s32[256]{0:T(256)S(1)}, u32[]{:S(2)}) copy-start(s32[256]{0:T(256)S(1)} %reshape.200) | copy-start | bytes 3076
  9.2 60.0 %copy-start.10 = (s32[1024]{0:T(1024)}, s32[1024]{0:T(1024)S(1)}, u32[]{:S(2)}) copy-start(s32[1024]{0:T(1024)S(1)} %pad_clamp_fusion) | copy-start | bytes 12292
  9.2 60.0 %copy-start.13 = (pred[256]{0:T(512)(128)(4,1)}, pred[256]{0:T(512)(128)(4,1)S(1)}, u32[]{:S(2)}) copy-start(pred[256]{0:T(512)(128)(4,1)S(1)} %compare_and_fusion) | copy-start | bytes 772
  9.9 84.1 %copy-start.7 = (pred[16,16]{1,0:T(8,128)(4,1)}, pred[16,16]{1,0:T(8,128)(4,1)S(1)}, u32[]{:S(2)}) copy-start(pred[16,16]{1,0:T(8,128)(4,1)S(1)} %get-tuple-element.182) | copy-start | bytes 772
  10.0 107.1 %copy-start.5 = (pred[16,16]{1,0:T(8,128)(4,1)}, pred[16,16]{1,0:T(8,128)(4,1)S(1)}, u32[]{:S(2)}) copy-start(pred[16,16]{1,0:T(8,128)(4,1)S(1)} %get-tuple-element.181) | copy-start | bytes 772
  145.4 4.3 collective-permute-start.1
  146.7 4.0 collective-permute-start
  150.9 20.9 %copy-start.1 = (f32[2,128,8,128]{3,2,1,0:T(8,128)S(1)}, f32[2,128,8,128]{3,2,1,0:T(8,128)}, u32[]{:S(2)}) copy-start(f32[2,128,8,128]{3,2,1,0:T(8,128)} %param.18) | copy-start | bytes 3145732
  150.9 20.8 %copy-start.9 = (f32[8]{0:T(128)S(1)}, f32[8]{0:T(128)}, u32[]{:S(2)}) copy-start(f32[8]{0:T(128)} %param.19) | copy-start | bytes 100
  151.9 9.1 %collective-permute-start.2 = (bf16[1152,64]{1,0:T(8,128)(2,1)}, bf16[1152,64]{1,0:T(8,128)(2,1)}, u32[]{:S(2)}, u32[]{:S(2)}) collective-permute-start(bf16[1152,64]{1,0:T(8,128)(2,1)} %get-tuple-element.178), channel_id=1, source_target_pairs={{0,1},{1,2},{2,3},{3,4},{4,5},{5,6},{6,7},{8,9},{9,10},{10,11},{11... | collective-permute-start | bytes 442376 | tf_op jit(solution)/shard_map/ppermute | solution.py:24
  155.1 11.3 %collective-permute-start.3 = (bf16[1152,64]{1,0:T(8,128)(2,1)}, bf16[1152,64]{1,0:T(8,128)(2,1)}, u32[]{:S(2)}, u32[]{:S(2)}) collective-permute-start(bf16[1152,64]{1,0:T(8,128)(2,1)} %get-tuple-element.177), channel_id=1, source_target_pairs={{1,0},{2,1},{3,2},{4,3},{5,4},{6,5},{7,6},{9,8},{10,9},{11,10},{12... | collective-permute-start | bytes 442376 | tf_op jit(solution)/shard_map/ppermute | solution.py:25
  252.7 4.5 copy-start.2
  320.9 4.5 copy-start.2
  389.1 4.5 copy-start.2
  457.4 4.5 copy-start.2
  467.7 3.5 copy-start.4
  491.1 12.0 %copy-start.8 = (pred[16,16]{1,0:T(8,128)(4,1)S(1)}, pred[16,16]{1,0:T(8,128)(4,1)}, u32[]{:S(2)}) copy-start(pred[16,16]{1,0:T(8,128)(4,1)} %copy-done.7) | copy-start | bytes 772
  514.0 13.2 %copy-start.6 = (pred[16,16]{1,0:T(8,128)(4,1)S(1)}, pred[16,16]{1,0:T(8,128)(4,1)}, u32[]{:S(2)}) copy-start(pred[16,16]{1,0:T(8,128)(4,1)} %copy-done.5) | copy-start | bytes 772
  537.1 7.9 %copy-start.12 = (s32[256]{0:T(256)S(1)}, s32[256]{0:T(256)}, u32[]{:S(2)}) copy-start(s32[256]{0:T(256)} %copy-done.11) | copy-start | bytes 3076
  549.9 100.2 %all-reduce.3.cloned.1.call-start = ((), (), s32[]{:S(2)}) async-start(), calls=%async_computation.4 | async-start | bytes 262144 | tf_op jit(solution)/shard_map/psum | solution.py:176
  617.0 76.1 %all-gather.5.cloned.1.call-start = ((), (), s32[]{:S(2)}) async-start(), calls=%async_computation.2 | async-start | bytes 1179648 | tf_op jit(solution)/shard_map/all_gather | solution.py:188
  694.5 4.8 copy-start.14
  (5 other events, 15.1 us)
Sparse Core Ops, SparseCore 0:
  10.1 51.7 all-gather.2
  550.0 66.9 reduce-scatter.1
  619.3 30.7 all-reduce.2
  652.8 40.2 all-gather.4
where the time goes:
time: 795 us; the launch traced here: 786 us
  matrix products  221 us (28%)
  local copies, waits for them, and re-layouts  208 us (26%)
  waiting for transfers between devices  196 us (25%)
  other arithmetic  111 us (14%)
  loops' own time  27.4 us (3%)
  between operations  14.3 us (2%)
  starting transfers between devices  8.95 us (1%)
    dot_general x48, matrix products, dot_plain(): return jnp.dot(left, right, preferred_element_type=jnp.float32)  105 us
    dot_general x32, matrix products, dot_right_t(): lax.dot_general(left, right, (((1,), (1,)), ((), ())), preferred_element_...  95 us
    reduce_scatter x1, waiting for transfers between devices, per_device(): lax.psum_scatter(whole_sum, 'col', scatter_dimension=0, tiled=True)  67.1 us
    all_gather x1, waiting for transfers between devices, per_device(): everything = lax.all_gather(masters, 'col', axis=0, tiled=True)  52 us
    rev x3, local copies, waits for them, and re-layouts, orient_cells(): cells = jnp.where(flip_second[..., None, None], cells[..., :, ::-1], cells)  39.6 us
    rev x3, local copies, waits for them, and re-layouts, orient_cells(): cells = jnp.where(flip_first[..., None, None], cells[..., ::-1, :], cells)  35.9 us
    psum x1, waiting for transfers between devices, per_device(): lax.psum(jnp.dot(selector, cell_grads, precision=lax.Precision.HIGHEST, p...  33 us
    all_gather x1, waiting for transfers between devices, per_device(): lax.all_gather(fresh.astype(jnp.bfloat16), 'col', axis=0, tiled=True)  32 us
  transfers between devices with their start and end apart: 8, of which 7 were waited for; matrix products, arithmetic and copies ran while one was open for 1% of the time, Pallas kernels for 0%

commit v1 on v0

--- a/solution.py
+++ b/solution.py
@@ -147,7 +147,14 @@
     masters, inst_master, inst_orient, owner_map, tile_free, target, kernel_spectra, socs_weights
 ):
     stored = masters.shape[0]
-    everything = lax.all_gather(masters, "col", axis=0, tiled=True)
+    ways, here, step = (lax.axis_size("col"), lax.axis_index("col"), masters.shape[0])
+    line, have = (masters, 1)
+    while have < ways:
+        line = jnp.concatenate(
+            [line, lax.ppermute(line, "col", [(d, (d - have) % ways) for d in range(ways)])], axis=0
+        )
+        have = 2 * have
+    everything = jnp.roll(line, here * step, axis=0)
     total_masters = everything.shape[0]
     matches = inst_master[..., None] == jnp.arange(total_masters, dtype=jnp.int32)
     slots = jnp.sum(jnp.where(matches, owner_map, 0), axis=-1)

time: 795 us -> 819 us (1.030)
  starting transfers between devices: 8.95 us -> 19.1 us
    ppermute x0 -> x3, waiting for transfers between devices: none -> 58.1 us  [per_device(): lax.ppermute(line, 'col', [(d, (d - have) % ways) for d in range(ways)])]
    all_gather x1 -> x0, waiting for transfers between devices: 52 us -> none  [per_device(): everything = lax.all_gather(masters, 'col', axis=0, tiled=True)]
  transfers between devices with their start and end apart: 8 -> 10, of which waited for: 7 -> 8; matrix products, arithmetic and copies ran while one was open for 1% -> 2% of each run, Pallas kernels for 0% -> 0%
where the time goes in v1:
time: 819 us; the launch traced here: 812 us
  matrix products  222 us (27%)
  local copies, waits for them, and re-layouts  216 us (26%)
  waiting for transfers between devices  199 us (24%)
  other arithmetic  113 us (14%)
  loops' own time  28.9 us (4%)
  starting transfers between devices  19.1 us (2%)
  between operations  14.3 us (2%)
    dot_general x48, matrix products, dot_plain(): return jnp.dot(left, right, preferred_element_type=jnp.float32)  105 us
    dot_general x32, matrix products, dot_right_t(): lax.dot_general(left, right, (((1,), (1,)), ((), ())), preferred_element_...  95 us
    reduce_scatter x1, waiting for transfers between devices, per_device(): lax.psum_scatter(whole_sum, 'col', scatter_dimension=0, tiled=True)  63.9 us
    ppermute x3, waiting for transfers between devices, per_device(): lax.ppermute(line, 'col', [(d, (d - have) % ways) for d in range(ways)])  58.1 us
    rev x3, local copies, waits for them, and re-layouts, orient_cells(): cells = jnp.where(flip_second[..., None, None], cells[..., :, ::-1], cells)  39.4 us
    rev x3, local copies, waits for them, and re-layouts, orient_cells(): cells = jnp.where(flip_first[..., None, None], cells[..., ::-1, :], cells)  35.7 us
    psum x1, waiting for transfers between devices, per_device(): lax.psum(jnp.dot(selector, cell_grads, precision=lax.Precision.HIGHEST, p...  32.8 us
    all_gather x1, waiting for transfers between devices, per_device(): lax.all_gather(fresh.astype(jnp.bfloat16), 'col', axis=0, tiled=True)  32 us
  transfers between devices with their start and end apart: 10, of which 8 were waited for; matrix products, arithmetic and copies ran while one was open for 2% of the time, Pallas kernels for 0%

profile of v1, /device:TPU:0, one launch (start us, length us, event | category | flops | bytes accessed | tf_op | source)
XLA Modules:
  0.0 811.6 jit_solution(13053092851475586162)
XLA Ops:
  23.3 9.7 %collective-permute-done.1 = f32[32,4096]{1,0:T(8,128)S(1)} collective-permute-done((f32[32,4096]{1,0:T(8,128)S(1)}, f32[32,4096]{1,0:T(8,128)S(1)}, u32[]{:S(2)}, u32[]{:S(2)}) %collective-permute-start.1) | collective-permute-done | bytes 524320 | tf_op jit(solution)/shard_map/ppermute | solution.py:154
  36.2 44.5 %collective-permute-done.2 = f32[64,4096]{1,0:T(8,128)S(1)} collective-permute-done((f32[64,4096]{1,0:T(8,128)S(1)}, f32[64,4096]{1,0:T(8,128)S(1)}, u32[]{:S(2)}, u32[]{:S(2)}) %collective-permute-start.2) | collective-permute-done | bytes 1048608 | tf_op jit(solution)/shard_map/ppermute | solution.py:154
  95.6 8.1 reshape.201
  103.6 11.9 %rev.18 = f32[16,16,64,64]{3,2,1,0:T(8,128)} reverse(f32[16,16,64,64]{3,2,1,0:T(8,128)} %reshape.201), dimensions={2} | reverse | bytes 8388608 | tf_op jit(solution)/shard_map/rev | solution.py:113
  115.5 9.8 %broadcast_select_fusion.2 = f32[16,16,64,64]{3,2,1,0:T(8,128)} fusion(f32[16,16,64,64]{3,2,1,0:T(8,128)} %rev.18, f32[16,16,64,64]{3,2,1,0:T(8,128)} %reshape.201, pred[16,16]{1,0:T(8,128)(4,1)S(1)} %get-tuple-element.182), kind=kLoop, calls=%fused_computation.136 | loop fusion | flops 1048576 | bytes 12583168 | tf_op jit(solution)/shard_map/jit(_where)/select_n | solution.py:113
  125.3 13.1 %rev.19 = f32[16,16,64,64]{3,2,1,0:T(8,128)} reverse(f32[16,16,64,64]{3,2,1,0:T(8,128)} %broadcast_select_fusion.2), dimensions={3} | reverse | bytes 8388608 | tf_op jit(solution)/shard_map/rev | solution.py:114
  144.8 9.8 %copy.21 = f32[16,64,16,64]{3,2,1,0:T(8,128)} copy(f32[16,64,16,64]{3,1,2,0:T(8,128)S(1)} %select_bitcast_fusion.1) | data formatting | bytes 8388608 | tf_op jit(solution)/shard_map/transpose | solution.py:123
  178.9 11.3 %collective-permute-done.5 = bf16[1152,64]{1,0:T(8,128)(2,1)S(1)} collective-permute-done((bf16[1152,64]{1,0:T(8,128)(2,1)S(1)}, bf16[1152,64]{1,0:T(8,128)(2,1)S(1)}, u32[]{:S(2)}, u32[]{:S(2)}) %collective-permute-start.5) | collective-permute-done | bytes 147488 | tf_op jit(solution)/shard_map/ppermute | solution.py:24
  194.2 296.6 %while.15 = (s32[]{:T(128)}, f32[4,512,512]{2,1,0:T(8,128)}, f32[4,512,512]{2,1,0:T(8,128)}, f32[8]{0:T(128)S(1)}, f32[2,128,8,128]{3,2,1,0:T(8,128)}, /*index=5...) while((s32[]{:T(128)}, f32[4,512,512]{2,1,0:T(8,128)}, ...), condition=%wide.region_5.7_spmd, body=%wide.region_1.6_spmd.sunk | while | flops 5924732928 | bytes 201381072 | solution.py:176
  510.5 9.2 %copy.45 = f32[16,64,16,64]{3,1,2,0:T(8,128)} copy(f32[16,64,16,64]{3,2,1,0:T(8,128)} %reshape.207) | data formatting | bytes 8388608 | tf_op jit(solution)/shard_map/reshape | solution.py:128
  519.7 11.9 %rev.20 = f32[16,16,64,64]{3,2,1,0:T(8,128)} reverse(f32[16,16,64,64]{3,2,1,0:T(8,128)} %bitcast.205), dimensions={2} | reverse | bytes 8388608 | tf_op jit(solution)/shard_map/rev | solution.py:113
  531.6 10.9 %broadcast_select_fusion.1 = f32[16,16,64,64]{3,2,1,0:T(8,128)} fusion(f32[16,16,64,64]{3,2,1,0:T(8,128)} %rev.20, pred[16,16]{1,0:T(8,128)(4,1)S(1)} %copy-done.9, f32[16,64,16,64]{3,2,1,0:T(8,128)} %reshape.207), kind=kLoop, calls=%fused_computation.135 | loop fusion | flops 1048576 | bytes 12583168 | tf_op jit(solution)/shard_map/jit(_where)/select_n | solution.py:113
  542.6 13.1 %rev.21 = f32[16,16,64,64]{3,2,1,0:T(8,128)} reverse(f32[16,16,64,64]{3,2,1,0:T(8,128)} %broadcast_select_fusion.1), dimensions={3} | reverse | bytes 8388608 | tf_op jit(solution)/shard_map/rev | solution.py:114
  555.7 9.8 %broadcast_select_fusion.3 = f32[16,16,64,64]{3,2,1,0:T(8,128)} fusion(f32[16,16,64,64]{3,2,1,0:T(8,128)} %rev.21, f32[16,16,64,64]{3,2,1,0:T(8,128)} %broadcast_select_fusion.1, pred[16,16]{1,0:T(8,128)(4,1)S(1)} %copy-done.7), kind=kLoop, calls=%fused_computation.137 | loop fusion | flops 1048576 | bytes 12583168 | tf_op jit(solution)/shard_map/jit(_where)/select_n | solution.py:114
  565.5 7.9 reshape.208
  578.3 63.9 %reduce-scatter.2.cloned.1.call-done = bf16[16,4096]{1,0:T(8,128)(2,1)} async-done(((bf16[128,4096]{1,0:T(8,128)(2,1)}), bf16[16,4096]{1,0:T(8,128)(2,1)}) %reduce-scatter.2.cloned.1.call-update) | async-done | bytes 131088 | tf_op jit(solution)/shard_map/reduce_scatter | solution.py:192
  642.6 32.8 %all-reduce.3.cloned.1.call-done = bf16[16,4096]{1,0:T(8,128)(2,1)} async-done(((bf16[16,4096]{1,0:T(8,128)(2,1)}), bf16[16,4096]{1,0:T(8,128)(2,1)}) %all-reduce.3.cloned.1.call-update) | async-done | bytes 131088 | tf_op jit(solution)/shard_map/psum | solution.py:183
  686.5 32.0 %all-gather.2.cloned.1.call-done = bf16[128,4096]{1,0:T(8,128)(2,1)} async-done(((bf16[16,4096]{1,0:T(8,128)(2,1)}), bf16[128,4096]{1,0:T(8,128)(2,1)}) %all-gather.2.cloned.1.call-update) | async-done | bytes 1048592 | tf_op jit(solution)/shard_map/all_gather | solution.py:195
  729.4 8.1 %reshape.210 = f32[16,16,64,64]{3,2,1,0:T(8,128)} reshape(f32[256,4096]{1,0:T(8,128)} %broadcast_select_fusion.4) | data formatting | bytes 8388608 | tf_op jit(solution)/shard_map/reshape | solution.py:121
  737.6 11.9 %rev.22 = f32[16,16,64,64]{3,2,1,0:T(8,128)} reverse(f32[16,16,64,64]{3,2,1,0:T(8,128)} %reshape.210), dimensions={2} | reverse | bytes 8388608 | tf_op jit(solution)/shard_map/rev | solution.py:113
  749.5 9.8 %broadcast_select_fusion = f32[16,16,64,64]{3,2,1,0:T(8,128)} fusion(f32[16,16,64,64]{3,2,1,0:T(8,128)} %rev.22, f32[16,16,64,64]{3,2,1,0:T(8,128)} %reshape.210, pred[16,16]{1,0:T(8,128)(4,1)S(1)} %copy-done.9), kind=kLoop, calls=%fused_computation.134 | loop fusion | flops 1048576 | bytes 12583168 | tf_op jit(solution)/shard_map/jit(_where)/select_n | solution.py:113
  759.3 13.1 %rev.23 = f32[16,16,64,64]{3,2,1,0:T(8,128)} reverse(f32[16,16,64,64]{3,2,1,0:T(8,128)} %broadcast_select_fusion), dimensions={3} | reverse | bytes 8388608 | tf_op jit(solution)/shard_map/rev | solution.py:114
  778.7 9.8 %copy.25 = f32[16,64,16,64]{3,2,1,0:T(8,128)} copy(f32[16,64,16,64]{3,1,2,0:T(8,128)S(1)} %select_bitcast_fusion) | data formatting | bytes 8388608 | tf_op jit(solution)/shard_map/transpose | solution.py:123
  796.1 8.6 %add_tanh_fusion = f32[1024,1024]{1,0:T(8,128)} fusion(f32[1024,1024]{1,0:T(8,128)} %reshape.211, f32[1024,1024]{1,0:T(8,128)} %param.16, f32[1024,1024]{1,0:T(8,128)} %subtract_multiply_fusion.2), kind=kLoop, calls=%fused_computation.131 | loop fusion | flops 2097152 | bytes 16777216 | tf_op jit(solution)/shard_map/tanh | solution.py:198
  (293 shorter events, 397.2 us)
Async XLA Ops:
  7.2 74.6 %copy-start.5 = (f32[16,4096]{1,0:T(8,128)S(1)}, f32[16,4096]{1,0:T(8,128)}, u32[]{:S(2)}) copy-start(f32[16,4096]{1,0:T(8,128)} %param.12) | copy-start | bytes 786436
  7.2 635.1 %reduce-scatter.2.cloned.1.call-start = ((), (), s32[]{:S(2)}) async-start(), calls=%async_computation.2 | async-start | bytes 1179648 | tf_op jit(solution)/shard_map/reduce_scatter | solution.py:192
  7.2 12.0 %collective-permute-start = (f32[16,4096]{1,0:T(8,128)}, f32[16,4096]{1,0:T(8,128)S(1)}, u32[]{:S(2)}, u32[]{:S(2)}) collective-permute-start(f32[16,4096]{1,0:T(8,128)} %param.12), channel_id=1, source_target_pairs={{0,7},{1,0},{2,1},{3,2},{4,3},{5,4},{6,5},{7,6},{8,15},{9,8},{10,9... | collective-permute-start | bytes 786440 | tf_op jit(solution)/shard_map/ppermute | solution.py:154
  14.5 20.0 %copy-start.12 = (s32[256]{0:T(256)}, s32[256]{0:T(256)S(1)}, u32[]{:S(2)}) copy-start(s32[256]{0:T(256)S(1)} %reshape.200) | copy-start | bytes 3076
  15.3 100.3 %copy-start.8 = (pred[16,16]{1,0:T(8,128)(4,1)}, pred[16,16]{1,0:T(8,128)(4,1)S(1)}, u32[]{:S(2)}) copy-start(pred[16,16]{1,0:T(8,128)(4,1)S(1)} %get-tuple-element.182) | copy-start | bytes 772
  15.3 123.2 %copy-start.6 = (pred[16,16]{1,0:T(8,128)(4,1)}, pred[16,16]{1,0:T(8,128)(4,1)S(1)}, u32[]{:S(2)}) copy-start(pred[16,16]{1,0:T(8,128)(4,1)S(1)} %get-tuple-element.181) | copy-start | bytes 772
  20.2 12.9 %collective-permute-start.1 = (f32[32,4096]{1,0:T(8,128)S(1)}, f32[32,4096]{1,0:T(8,128)S(1)}, u32[]{:S(2)}, u32[]{:S(2)}) collective-permute-start(f32[32,4096]{1,0:T(8,128)S(1)} %pad_maximum_fusion.2), channel_id=1, source_target_pairs={{0,6},{1,7},{2,0},{3,1},{4,2},{5,3},{6,4},{7,5},{8,14},{9,15},{10,... | collective-permute-start | bytes 1572872 | tf_op jit(solution)/shard_map/ppermute | solution.py:154
  34.1 46.6 %collective-permute-start.2 = (f32[64,4096]{1,0:T(8,128)S(1)}, f32[64,4096]{1,0:T(8,128)S(1)}, u32[]{:S(2)}, u32[]{:S(2)}) collective-permute-start(f32[64,4096]{1,0:T(8,128)S(1)} %pad_maximum_fusion.1), channel_id=1, source_target_pairs={{0,4},{1,5},{2,6},{3,7},{4,0},{5,1},{6,2},{7,3},{8,12},{9,13},{10,... | collective-permute-start | bytes 3145736 | tf_op jit(solution)/shard_map/ppermute | solution.py:154
  34.5 56.2 %copy-start.14 = (pred[256]{0:T(512)(128)(4,1)}, pred[256]{0:T(512)(128)(4,1)S(1)}, u32[]{:S(2)}) copy-start(pred[256]{0:T(512)(128)(4,1)S(1)} %compare_and_fusion) | copy-start | bytes 772
  34.6 52.3 %copy-start.11 = (s32[1024]{0:T(1024)}, s32[1024]{0:T(1024)S(1)}, u32[]{:S(2)}) copy-start(s32[1024]{0:T(1024)S(1)} %pad_clamp_fusion) | copy-start | bytes 12292
  166.8 4.3 collective-permute-start.4
  168.1 4.0 collective-permute-start.3
  172.3 21.9 %copy-start.10 = (f32[8]{0:T(128)S(1)}, f32[8]{0:T(128)}, u32[]{:S(2)}) copy-start(f32[8]{0:T(128)} %param.19) | copy-start | bytes 100
  172.5 17.7 %collective-permute-start.5 = (bf16[1152,64]{1,0:T(8,128)(2,1)S(1)}, bf16[1152,64]{1,0:T(8,128)(2,1)S(1)}, u32[]{:S(2)}, u32[]{:S(2)}) collective-permute-start(bf16[1152,64]{1,0:T(8,128)(2,1)S(1)} %get-tuple-element.178), channel_id=1, source_target_pairs={{0,1},{1,2},{2,3},{3,4},{4,5},{5,6},{6,7},{8,9},{9,10},{10,11},{11... | collective-permute-start | bytes 442376 | tf_op jit(solution)/shard_map/ppermute | solution.py:24
  177.6 12.6 %collective-permute-start.6 = (bf16[1152,64]{1,0:T(8,128)(2,1)S(1)}, bf16[1152,64]{1,0:T(8,128)(2,1)S(1)}, u32[]{:S(2)}, u32[]{:S(2)}) collective-permute-start(bf16[1152,64]{1,0:T(8,128)(2,1)S(1)} %get-tuple-element.177), channel_id=1, source_target_pairs={{1,0},{2,1},{3,2},{4,3},{5,4},{6,5},{7,6},{9,8},{10,9},{11,10},{12... | collective-permute-start | bytes 442376 | tf_op jit(solution)/shard_map/ppermute | solution.py:25
  230.5 5.1 copy-start.2
  300.3 5.1 copy-start.2
  370.1 5.1 copy-start.2
  439.9 5.1 copy-start.2
  519.7 11.9 %copy-start.9 = (pred[16,16]{1,0:T(8,128)(4,1)S(1)}, pred[16,16]{1,0:T(8,128)(4,1)}, u32[]{:S(2)}) copy-start(pred[16,16]{1,0:T(8,128)(4,1)} %copy-done.8) | copy-start | bytes 772
  542.5 13.1 %copy-start.7 = (pred[16,16]{1,0:T(8,128)(4,1)S(1)}, pred[16,16]{1,0:T(8,128)(4,1)}, u32[]{:S(2)}) copy-start(pred[16,16]{1,0:T(8,128)(4,1)} %copy-done.6) | copy-start | bytes 772
  565.5 7.9 copy-start.13
  578.3 97.1 %all-reduce.3.cloned.1.call-start = ((), (), s32[]{:S(2)}) async-start(), calls=%async_computation.3 | async-start | bytes 262144 | tf_op jit(solution)/shard_map/psum | solution.py:183
  642.3 76.1 %all-gather.2.cloned.1.call-start = ((), (), s32[]{:S(2)}) async-start(), calls=%async_computation.1 | async-start | bytes 1179648 | tf_op jit(solution)/shard_map/all_gather | solution.py:195
  (11 other events, 31.7 us)
Sparse Core Ops, SparseCore 0:
  578.4 63.8 reduce-scatter.1
  644.6 30.7 all-reduce.2
  678.1 40.2 all-gather.1
